TPU v7x, 256 devices: a whole 4x4x8 slice. The times are simulated.
256 devices in a mesh: grp: 4 (over y), seq: 64 (over z, x, core).
Axes of the slice: x: 4, y: 4, z: 8, core: 2. Of those that a mesh axis runs over, the one named last changes fastest.
Arguments:
- tokens: bfloat16 [1024, 1024], P(('grp', 'seq')), may hold values from -6 to 6
- attn_gain: float32 [1024], replicated, may hold values from 0.1 to 1.9
- w_qkv: bfloat16 [1024, 3072], replicated, may hold values from -0.1875 to 0.1875
- w_out: bfloat16 [1024, 1024], replicated, may hold values from -0.1875 to 0.1875
- mlp_gain: float32 [1024], replicated, may hold values from 0.1 to 1.9
- w_gate_up: bfloat16 [2, 1024, 4096], P(None, None, 'seq'), may hold values from -0.1875 to 0.1875
- w_down: bfloat16 [4096, 1024], P('seq'), may hold values from -0.09375 to 0.09375
- kv_cache: bfloat16 [3072, 2, 64, 1024], P(('grp', 'seq'))
- block_owner: int32 [3072], P(('grp', 'seq')), may hold values from 0 to 255, as said below
- block_fill: int32 [3072], P(('grp', 'seq')), may hold values from 0 to 64, as said below
Outputs:
- output: bfloat16 [1024, 1024], P(('grp', 'seq'))
Inputs may be any that keep to these rules, and one draw needn't show every extreme that they name: `block_fill`: each request has at least one block; in each group one request fills exactly 256 whole blocks, every other has at most 2 blocks; blocks of one request are live from their start and all but its last are full; blocks with no live token exist in every group. `block_owner`: every served request number of a group names some block of that group.
All inputs are finite; a program needn't handle non-finite values.
Results may differ from a plain program's by a relative error of at most 0.024.
Values may be sent and summed in bfloat16 or wider, within the bound.
No kernel may reach another device: no remote copies, remote signals or barrier semaphores. Data moves between devices by JAX's collectives and lax.ppermute only.
A program may use at most 320 MiB of HBM per device.

v0:
```python
import jax
import jax.numpy as jnp
from jax import lax
from jax.sharding import PartitionSpec as P

HEADS = 16
floor_score = -1e30
epsilon = 1e-05


def rms_scaled(row_data, gain):
    values = row_data.astype(jnp.float32)
    return values * lax.rsqrt(jnp.mean(values * values, axis=-1, keepdims=True) + epsilon) * gain


def body(
    tokens, attn_gain, w_qkv, w_out, mlp_gain, w_gate_up, w_down, kv_cache, block_owner, block_fill
):
    groups = lax.axis_size("grp")
    row_count, feature_count = tokens.shape
    head_count = HEADS
    head_dim = feature_count // head_count
    per_group = row_count // groups
    score_scale = head_dim ** (-0.5)
    normed = rms_scaled(tokens, attn_gain).astype(jnp.bfloat16)
    qkv = jnp.dot(normed, w_qkv, preferred_element_type=jnp.float32).astype(jnp.bfloat16)
    sent_qkv, sent_input = (
        lax.all_to_all(
            qkv.reshape(per_group, groups, 3 * feature_count),
            "grp",
            split_axis=1,
            concat_axis=1,
            tiled=True,
        ),
        lax.all_to_all(
            tokens.reshape(per_group, groups, feature_count),
            "grp",
            split_axis=1,
            concat_axis=1,
            tiled=True,
        ),
    )
    served_qkv = sent_qkv.reshape(row_count, 3 * feature_count)
    served_input = sent_input.reshape(row_count, feature_count)
    query_own = served_qkv[:, :feature_count]
    key_own = served_qkv[:, feature_count : 2 * feature_count]
    value_own = served_qkv[:, 2 * feature_count :]
    offset = lax.axis_index("seq") * row_count
    query_all = lax.all_gather(query_own, "seq", axis=0, tiled=True)
    group_rows = query_all.shape[0]
    blocks, _, span, _ = kv_cache.shape
    key_block = kv_cache[:, 0].reshape(blocks, span, head_count, head_dim)
    value_block = kv_cache[:, 1].reshape(blocks, span, head_count, head_dim)
    query_blocks = query_all[block_owner].reshape(blocks, head_count, head_dim)
    scores = (
        jnp.einsum("bhd,bthd->bht", query_blocks, key_block, preferred_element_type=jnp.float32)
        * score_scale
    )
    is_valid = (
        lax.broadcasted_iota(jnp.int32, (blocks, head_count, span), 2) < block_fill[:, None, None]
    )
    masked = jnp.where(is_valid, scores, floor_score)
    block_max = jnp.max(masked, axis=2)
    weights = jnp.where(is_valid, jnp.exp(masked - block_max[:, :, None]), 0.0).astype(jnp.bfloat16)
    block_total = jnp.sum(weights.astype(jnp.float32), axis=2)
    block_sum = jnp.einsum(
        "bht,bthd->bhd", weights, value_block, preferred_element_type=jnp.float32
    )
    member = block_owner[None, :] == lax.broadcasted_iota(jnp.int32, (group_rows, blocks), 0)
    local_max = jnp.max(jnp.where(member[:, :, None], block_max[None, :, :], floor_score), axis=1)
    factor = jnp.exp(block_max - local_max[block_owner])
    member_table = member.astype(jnp.float32)
    local_total = jnp.dot(member_table, block_total * factor, precision=lax.Precision.HIGHEST)
    local_sum = jnp.dot(
        member_table,
        (block_sum * factor[:, :, None]).reshape(blocks, feature_count),
        precision=lax.Precision.HIGHEST,
    )
    own_max = lax.dynamic_slice_in_dim(local_max, offset, row_count, 0)
    own_total = lax.dynamic_slice_in_dim(local_total, offset, row_count, 0)
    own_sum = lax.dynamic_slice_in_dim(local_sum, offset, row_count, 0)
    query_float = query_own.astype(jnp.float32).reshape(row_count, head_count, head_dim)
    key_float = key_own.astype(jnp.float32).reshape(row_count, head_count, head_dim)
    own_score = jnp.sum(query_float * key_float, axis=2) * score_scale
    joined = jnp.maximum(own_max, own_score)
    keep_weight = jnp.exp(own_max - joined)
    own_weight = jnp.exp(own_score - joined)
    new_total = own_total * keep_weight + own_weight
    new_sum = own_sum.reshape(row_count, head_count, head_dim) * keep_weight[:, :, None]
    new_sum = (
        new_sum
        + value_own.astype(jnp.float32).reshape(row_count, head_count, head_dim)
        * own_weight[:, :, None]
    )
    local_max = lax.dynamic_update_slice_in_dim(local_max, joined, offset, 0)
    local_total = lax.dynamic_update_slice_in_dim(local_total, new_total, offset, 0)
    local_sum = lax.dynamic_update_slice_in_dim(
        local_sum, new_sum.reshape(row_count, feature_count), offset, 0
    )
    local_max, local_total, local_sum = (local_max, local_total, local_sum)
    maxima = lax.pmax(local_max, "seq")
    factor = jnp.exp(local_max - maxima)
    scaled_sum = (
        local_sum.reshape(local_sum.shape[0], head_count, head_dim) * factor[:, :, None]
    ).reshape(local_sum.shape)
    totals, weighted = (
        lax.psum_scatter(local_total * factor, "seq", scatter_dimension=0, tiled=True),
        lax.psum_scatter(scaled_sum, "seq", scatter_dimension=0, tiled=True),
    )
    scaled = weighted.reshape(weighted.shape[0], head_count, head_dim) / totals[:, :, None]
    context = scaled.reshape(weighted.shape[0], feature_count).astype(jnp.bfloat16)
    mixed_rows = served_input.astype(jnp.float32) + jnp.dot(
        context, w_out, preferred_element_type=jnp.float32
    )
    normed_mlp = rms_scaled(mixed_rows, mlp_gain).astype(jnp.bfloat16)
    rows_piece = lax.all_gather(normed_mlp, "seq", axis=0, tiled=True)
    gate_part = jnp.dot(rows_piece, w_gate_up[0], preferred_element_type=jnp.float32)
    up_part = jnp.dot(rows_piece, w_gate_up[1], preferred_element_type=jnp.float32)
    hidden = (jax.nn.silu(gate_part) * up_part).astype(jnp.bfloat16)
    partial_value = jnp.dot(hidden, w_down, preferred_element_type=jnp.float32)
    residual, partial_value = (mixed_rows, partial_value)
    down_sum = lax.psum_scatter(partial_value, "seq", scatter_dimension=0, tiled=True)
    output = (residual + down_sum).astype(jnp.bfloat16)
    returned = lax.all_to_all(
        output.reshape(per_group, groups, feature_count),
        "grp",
        split_axis=1,
        concat_axis=1,
        tiled=True,
    )
    return returned.reshape(row_count, feature_count)


def solution(mesh):
    in_specs = (
        P(("grp", "seq"), None),
        P(),
        P(),
        P(),
        P(),
        P(None, None, "seq"),
        P("seq", None),
        P(("grp", "seq"), None, None, None),
        P(("grp", "seq")),
        P(("grp", "seq")),
    )
    out_specs = P(("grp", "seq"), None)
    return jax.shard_map(body, mesh=mesh, in_specs=in_specs, out_specs=out_specs, check_vma=False)
```

profile of v0, /device:TPU:2, one launch (start us, length us, event | category | flops | bytes accessed | tf_op | source)
XLA Modules:
  0.0 860.8 jit_solution(14917239014895460157)
XLA Ops:
  6.5 1.0 fusion.20
  7.5 3.8 fusion
  11.4 0.5 broadcast.73
  11.8 0.7 reduce
  12.5 0.6 reshape.124
  13.1 4.5 all-to-all-start.1
  17.6 0.1 iota_compare_fusion.1
  17.7 4.0 fusion.39
  21.7 4.1 copy.67
  25.8 5.3 reshape_squeeze.7
  31.1 52.9 %all-gather = bf16[64,4,1024]{2,1,0:T(4,128)(2,1)S(1)} all-gather(bf16[1,4,1024]{2,1,0:T(4,128)(2,1)S(1)} %slice_bitcast_fusion), channel_id=1, replica_groups=mesh['grp'=4,'seq'=64] {'seq'}, dimensions={0}, use_global_device_ids=true | all-gather | bytes 532480 | tf_op jit(solution)/shard_map/all_gather | solution.py:49
  84.0 0.1 reshape.110
  84.1 0.6 gather_fusion
  84.7 0.1 reshape.118
  84.8 2.8 fusion.40
  87.6 0.2 fusion.13
  87.8 0.2 convert_reduce_fusion
  88.0 0.1 select_reduce_fusion
  88.1 0.1 copy.53
  88.2 0.6 gather_fusion.1
  88.8 0.2 fusion.25
  89.0 0.1 constant_dynamic-slice_fusion.1
  89.1 0.1 copy.72
  89.2 0.1 mul.127
  89.3 0.1 reduce_sum.37
  89.4 0.1 mul.130
  89.4 0.1 mul.131
  89.5 0.1 mul.133
  89.6 0.1 mul.134
  89.7 2.8 fusion.1
  92.5 0.1 broadcast_multiply_fusion
  92.6 0.1 reshape.87
  92.7 0.7 fusion.26
  93.4 0.1 copy.58
  93.5 0.3 dynamic_update_slice.11
  93.8 0.1 copy.55
  93.8 0.3 dynamic_update_slice.10
  94.1 244.1 %pmax.7 = f32[256,16]{0,1:T(8,128)S(1)} all-reduce(f32[256,16]{0,1:T(8,128)S(1)} %dynamic_update_slice.10), channel_id=1, replica_groups=mesh['grp'=4,'seq'=64] {'seq'}, use_global_device_ids=true, to_apply=%region_4.5 | all-reduce | flops 4096 | bytes 32768 | tf_op jit(solution)/shard_map/pmax | solution.py:101
  338.2 0.6 fusion.38
  338.8 1.1 mul.136
  339.8 2.6 copy.56
  342.5 2.4 mul.138
  344.9 0.0 all-reduce.6.cloned.1.call-update
  344.9 0.6 reduce.1
  345.6 0.6 reshape.126
  346.2 4.8 all-to-all-start
  351.0 0.6 dynamic-slice
  352.2 4.1 all-to-all-done
  356.3 246.3 %all-reduce.1 = f32[256,16]{0,1:T(8,128)S(1)} all-reduce(f32[256,16]{0,1:T(8,128)} %get-tuple-element.5), channel_id=3, replica_groups=mesh['grp'=4,'seq'=64] {'seq'}, use_global_device_ids=true, to_apply=%region_7.8.clone | all-reduce | flops 4096 | bytes 32768
  602.6 0.1 constant_dynamic-slice_fusion
  602.7 0.1 copy.59
  602.7 0.1 div.22
  602.8 0.1 div.23
  602.9 1.3 multiply_reduce_fusion
  604.2 0.1 fusion.28
  604.3 52.7 %all-gather.1 = bf16[64,4,1024]{2,1,0:T(4,128)(2,1)S(1)} all-gather(bf16[1,4,1024]{2,1,0:T(4,128)(2,1)S(1)} %fusion.28), channel_id=1, replica_groups=mesh['grp'=4,'seq'=64] {'seq'}, dimensions={0}, use_global_device_ids=true | all-gather | bytes 532480 | tf_op jit(solution)/shard_map/all_gather | solution.py:116
  657.0 0.1 reshape.112
  657.1 0.3 fusion.7
  657.4 1.9 fusion.4
  659.3 183.2 %all-reduce.8.cloned.1.call-done = f32[256,1024]{1,0:T(8,128)} async-done(((f32[256,1024]{1,0:T(8,128)}), f32[256,1024]{1,0:T(8,128)}) %all-reduce.8.cloned.1.call-update) | async-done | bytes 1048592
  842.5 0.8 fusion.29
  843.3 0.6 reduce.2
  843.9 9.4 %all_to_all.15 = bf16[4,2,512]{2,1,0:T(2,128)(2,1)S(1)} all-to-all(bf16[4,2,512]{2,1,0:T(2,128)(2,1)S(1)} %reshape.128), channel_id=1, replica_groups=mesh['grp'=4,'seq'=64] {'grp'}, dimensions={0} | all-to-all | bytes 16384 | tf_op jit(solution)/shard_map/all_to_all | solution.py:124
  853.3 0.6 copy.84
  (38 shorter events, 0.3 us)
Async XLA Ops:
  6.5 596.4 %copy-start = (bf16[1024,1024]{1,0:T(8,128)(2,1)S(1)}, bf16[1024,1024]{1,0:T(8,128)(2,1)}, u32[]{:S(2)}) copy-start(bf16[1024,1024]{1,0:T(8,128)(2,1)} %param.13) | copy-start | bytes 6291460
  7.5 10.1 %copy-start.6 = (s32[12]{0:T(128)S(1)}, s32[12]{0:T(128)}, u32[]{:S(2)}) copy-start(s32[12]{0:T(128)} %param.18) | copy-start | bytes 148
  13.1 17.9 %all-to-all-start.1 = ((bf16[4,2,1536]{2,1,0:T(2,128)(2,1)}), bf16[4,2,1536]{2,1,0:T(2,128)(2,1)S(1)}, u32[]{:S(2)}, u32[]{:S(2)}) async-start(bf16[4,2,1536]{2,1,0:T(2,128)(2,1)} %reshape.124), calls=%async_computation.1 | async-start | bytes 49152 | tf_op jit(solution)/shard_map/all_to_all | solution.py:28
  17.6 585.3 %all-reduce.6.cloned.1.call-start = ((), (), s32[]{:S(2)}) async-start(), calls=%async_computation.3 | async-start | bytes 2097152
  31.1 56.6 %copy-start.5 = (s32[12]{0:T(128)S(1)}, s32[12]{0:T(128)}, u32[]{:S(2)}) copy-start(s32[12]{0:T(128)} %param.19) | copy-start | bytes 148
  339.8 5.1 copy-start.3
  339.8 11.2 %copy-start.7 = (u32[256]{0:T(256)S(1)}, u32[256]{0:T(256)}, u32[]{:S(2)}) copy-start(u32[256]{0:T(256)} %constant.36) | copy-start | bytes 3076
  344.9 259.3 %copy-start.4 = (f32[1024]{0:T(1024)S(1)}, f32[1024]{0:T(1024)}, u32[]{:S(2)}) copy-start(f32[1024]{0:T(1024)} %param.14) | copy-start | bytes 12292
  344.9 312.2 %copy-start.1 = (bf16[2,1024,64]{1,2,0:T(8,128)(2,1)S(1)}, bf16[2,1024,64]{1,2,0:T(8,128)(2,1)}, u32[]{:S(2)}) copy-start(bf16[2,1024,64]{1,2,0:T(8,128)(2,1)} %param.15) | copy-start | bytes 786436
  344.9 312.5 %copy-start.2 = (bf16[64,1024]{1,0:T(8,128)(2,1)S(1)}, bf16[64,1024]{1,0:T(8,128)(2,1)}, u32[]{:S(2)}) copy-start(bf16[64,1024]{1,0:T(8,128)(2,1)} %param.16) | copy-start | bytes 393220
  346.2 10.1 %all-to-all-start = ((bf16[4,2,512]{2,1,0:T(2,128)(2,1)}), bf16[4,2,512]{2,1,0:T(2,128)(2,1)S(1)}, u32[]{:S(2)}, u32[]{:S(2)}) async-start(bf16[4,2,512]{2,1,0:T(2,128)(2,1)} %reshape.126), calls=%async_computation | async-start | bytes 16384 | tf_op jit(solution)/shard_map/all_to_all | solution.py:35
  351.0 491.5 %all-reduce.8.cloned.1.call-start = ((), (), s32[]{:S(2)}) async-start(), calls=%async_computation.4 | async-start | bytes 2097152
Sparse Core Ops, SparseCore 0:
  345.0 188.2 all-reduce.5
  659.4 183.0 all-reduce.7
where the time goes:
time: 862 us; the launch traced here: 861 us
  blocking collectives  605 us (70%)
  waiting for transfers between devices  187 us (22%)
  local copies, waits for them, and re-layouts  23.4 us (3%)
  between operations  14.3 us (2%)
  matrix products  13.7 us (2%)
  starting transfers between devices  9.26 us (1%)
    unnamed x1, blocking collectives  246 us
    pmax x1, blocking collectives, body(): maxima = lax.pmax(local_max, 'seq')  244 us
    unnamed x4, waiting for transfers between devices  183 us
    all_gather x1, blocking collectives, body(): query_all = lax.all_gather(query_own, 'seq', axis=0, tiled=True)  52.9 us
    all_gather x1, blocking collectives, body(): rows_piece = lax.all_gather(normed_mlp, 'seq', axis=0, tiled=True)  52.7 us
  transfers between devices with their start and end apart: 4, of which 2 were waited for; matrix products, arithmetic and copies ran while one was open for 2% of the time, Pallas kernels for 0%

commit v1 on v0

--- a/solution.py
+++ b/solution.py
@@ -113,7 +113,9 @@
         context, w_out, preferred_element_type=jnp.float32
     )
     normed_mlp = rms_scaled(mixed_rows, mlp_gain).astype(jnp.bfloat16)
-    rows_piece = lax.all_gather(normed_mlp, "seq", axis=0, tiled=True)
+    rows_piece = jnp.concatenate(
+        lax.all_to_all(jnp.stack([normed_mlp] * lax.axis_size("seq")), "seq", 0, 0), axis=0
+    )
     gate_part = jnp.dot(rows_piece, w_gate_up[0], preferred_element_type=jnp.float32)
     up_part = jnp.dot(rows_piece, w_gate_up[1], preferred_element_type=jnp.float32)
     hidden = (jax.nn.silu(gate_part) * up_part).astype(jnp.bfloat16)

time: 862 us -> 835 us (0.969)
  blocking collectives: 605 us -> 582 us
    all_gather x1 -> x0, blocking collectives: 52.7 us -> none  [body(): rows_piece = lax.all_gather(normed_mlp, 'seq', axis=0, tiled=True)]
    all_to_all x0 -> x1, blocking collectives: none -> 29.1 us  [body(): lax.all_to_all(jnp.stack([normed_mlp] * lax.axis_size('seq')), 'seq', 0, 0)]
where the time goes in v1:
time: 835 us; the launch traced here: 834 us
  blocking collectives  582 us (70%)
  waiting for transfers between devices  184 us (22%)
  local copies, waits for them, and re-layouts  23.5 us (3%)
  between operations  14.3 us (2%)
  matrix products  13.7 us (2%)
  starting transfers between devices  9.26 us (1%)
    unnamed x1, blocking collectives  246 us
    pmax x1, blocking collectives, body(): maxima = lax.pmax(local_max, 'seq')  244 us
    unnamed x4, waiting for transfers between devices  180 us
    all_gather x1, blocking collectives, body(): query_all = lax.all_gather(query_own, 'seq', axis=0, tiled=True)  52.9 us
    all_to_all x1, blocking collectives, body(): lax.all_to_all(jnp.stack([normed_mlp] * lax.axis_size('seq')), 'seq', 0, 0)  29.1 us
  transfers between devices with their start and end apart: 4, of which 2 were waited for; matrix products, arithmetic and copies ran while one was open for 2% of the time, Pallas kernels for 0%

profile of v1, /device:TPU:2, one launch (start us, length us, event | category | flops | bytes accessed | tf_op | source)
XLA Modules:
  0.0 834.3 jit_solution(6617653073184084321)
XLA Ops:
  6.5 1.0 fusion.20
  7.5 3.8 fusion
  11.4 0.5 broadcast.75
  11.8 0.7 reduce
  12.5 0.6 reshape.128
  13.1 4.5 all-to-all-start.1
  17.6 0.1 iota_compare_fusion.1
  17.7 4.0 fusion.38
  21.7 4.1 copy.67
  25.8 5.3 reshape_squeeze.7
  31.1 52.9 %all-gather = bf16[64,4,1024]{2,1,0:T(4,128)(2,1)S(1)} all-gather(bf16[1,4,1024]{2,1,0:T(4,128)(2,1)S(1)} %slice_bitcast_fusion), channel_id=1, replica_groups=mesh['grp'=4,'seq'=64] {'seq'}, dimensions={0}, use_global_device_ids=true | all-gather | bytes 532480 | tf_op jit(solution)/shard_map/all_gather | solution.py:49
  84.0 0.1 reshape.116
  84.1 0.6 gather_fusion
  84.7 0.1 reshape.122
  84.8 2.8 fusion.39
  87.6 0.2 fusion.13
  87.8 0.2 convert_reduce_fusion
  88.0 0.1 select_reduce_fusion
  88.1 0.1 copy.53
  88.2 0.6 gather_fusion.1
  88.8 0.2 fusion.25
  89.0 0.1 constant_dynamic-slice_fusion.1
  89.1 0.1 copy.72
  89.2 0.1 mul.127
  89.3 0.1 reduce_sum.37
  89.4 0.1 mul.130
  89.4 0.1 mul.131
  89.5 0.1 mul.133
  89.6 0.1 mul.134
  89.7 2.8 fusion.1
  92.5 0.1 broadcast_multiply_fusion
  92.6 0.1 reshape.92
  92.7 0.7 fusion.26
  93.4 0.1 copy.58
  93.5 0.3 dynamic_update_slice.11
  93.8 0.1 copy.55
  93.8 0.3 dynamic_update_slice.10
  94.1 244.1 %pmax.7 = f32[256,16]{0,1:T(8,128)S(1)} all-reduce(f32[256,16]{0,1:T(8,128)S(1)} %dynamic_update_slice.10), channel_id=1, replica_groups=mesh['grp'=4,'seq'=64] {'seq'}, use_global_device_ids=true, to_apply=%region_4.5 | all-reduce | flops 4096 | bytes 32768 | tf_op jit(solution)/shard_map/pmax | solution.py:101
  338.2 0.6 fusion.37
  338.8 1.1 mul.136
  339.8 2.6 copy.56
  342.5 2.4 mul.138
  345.0 0.7 reduce.1
  345.6 0.6 reshape.130
  346.2 4.8 all-to-all-start
  351.0 0.6 dynamic-slice
  352.3 4.1 all-to-all-done
  356.4 246.2 %all-reduce.1 = f32[256,16]{0,1:T(8,128)S(1)} all-reduce(f32[256,16]{0,1:T(8,128)} %get-tuple-element.5), channel_id=3, replica_groups=mesh['grp'=4,'seq'=64] {'seq'}, use_global_device_ids=true, to_apply=%region_7.8.clone | all-reduce | flops 4096 | bytes 32768
  602.6 0.1 constant_dynamic-slice_fusion
  602.7 0.1 copy.59
  602.7 0.1 div.22
  602.8 0.1 div.23
  602.9 1.3 multiply_reduce_fusion
  604.2 0.1 multiply_convert_fusion
  604.3 0.1 stack.2
  604.4 29.1 %all_to_all.20 = bf16[64,4,1024]{2,1,0:T(4,128)(2,1)S(1)} all-to-all(bf16[64,4,1024]{2,1,0:T(4,128)(2,1)S(1)} %stack.2), channel_id=1, replica_groups=mesh['grp'=4,'seq'=64] {'seq'}, dimensions={0} | all-to-all | bytes 1048576 | tf_op jit(solution)/shard_map/all_to_all | solution.py:117
  633.5 0.1 reshape.93
  633.7 0.3 fusion.7
  634.0 1.9 fusion.4
  635.9 180.1 %all-reduce.8.cloned.1.call-done = f32[256,1024]{1,0:T(8,128)} async-done(((f32[256,1024]{1,0:T(8,128)}), f32[256,1024]{1,0:T(8,128)}) %all-reduce.8.cloned.1.call-update) | async-done | bytes 1048592
  816.0 0.8 fusion.28
  816.8 0.6 reduce.2
  817.4 9.4 %all_to_all.21 = bf16[4,2,512]{2,1,0:T(2,128)(2,1)S(1)} all-to-all(bf16[4,2,512]{2,1,0:T(2,128)(2,1)S(1)} %reshape.132), channel_id=1, replica_groups=mesh['grp'=4,'seq'=64] {'grp'}, dimensions={0} | all-to-all | bytes 16384 | tf_op jit(solution)/shard_map/all_to_all | solution.py:126
  826.8 0.6 copy.84
  (39 shorter events, 0.3 us)
Async XLA Ops:
  6.5 596.4 %copy-start = (bf16[1024,1024]{1,0:T(8,128)(2,1)S(1)}, bf16[1024,1024]{1,0:T(8,128)(2,1)}, u32[]{:S(2)}) copy-start(bf16[1024,1024]{1,0:T(8,128)(2,1)} %param.13) | copy-start | bytes 6291460
  7.5 10.1 %copy-start.6 = (s32[12]{0:T(128)S(1)}, s32[12]{0:T(128)}, u32[]{:S(2)}) copy-start(s32[12]{0:T(128)} %param.18) | copy-start | bytes 148
  13.1 17.9 %all-to-all-start.1 = ((bf16[4,2,1536]{2,1,0:T(2,128)(2,1)}), bf16[4,2,1536]{2,1,0:T(2,128)(2,1)S(1)}, u32[]{:S(2)}, u32[]{:S(2)}) async-start(bf16[4,2,1536]{2,1,0:T(2,128)(2,1)} %reshape.128), calls=%async_computation.1 | async-start | bytes 49152 | tf_op jit(solution)/shard_map/all_to_all | solution.py:28
  17.6 585.3 %all-reduce.6.cloned.1.call-start = ((), (), s32[]{:S(2)}) async-start(), calls=%async_computation.4 | async-start | bytes 2097152
  31.1 56.6 %copy-start.5 = (s32[12]{0:T(128)S(1)}, s32[12]{0:T(128)}, u32[]{:S(2)}) copy-start(s32[12]{0:T(128)} %param.19) | copy-start | bytes 148
  339.8 5.1 copy-start.3
  339.8 11.2 %copy-start.7 = (u32[256]{0:T(256)S(1)}, u32[256]{0:T(256)}, u32[]{:S(2)}) copy-start(u32[256]{0:T(256)} %constant.36) | copy-start | bytes 3076
  344.9 259.3 %copy-start.4 = (f32[1024]{0:T(1024)S(1)}, f32[1024]{0:T(1024)}, u32[]{:S(2)}) copy-start(f32[1024]{0:T(1024)} %param.14) | copy-start | bytes 12292
  344.9 288.8 %copy-start.1 = (bf16[2,1024,64]{1,2,0:T(8,128)(2,1)S(1)}, bf16[2,1024,64]{1,2,0:T(8,128)(2,1)}, u32[]{:S(2)}) copy-start(bf16[2,1024,64]{1,2,0:T(8,128)(2,1)} %param.15) | copy-start | bytes 786436
  344.9 289.1 %copy-start.2 = (bf16[64,1024]{1,0:T(8,128)(2,1)S(1)}, bf16[64,1024]{1,0:T(8,128)(2,1)}, u32[]{:S(2)}) copy-start(bf16[64,1024]{1,0:T(8,128)(2,1)} %param.16) | copy-start | bytes 393220
  346.2 10.1 %all-to-all-start = ((bf16[4,2,512]{2,1,0:T(2,128)(2,1)}), bf16[4,2,512]{2,1,0:T(2,128)(2,1)S(1)}, u32[]{:S(2)}, u32[]{:S(2)}) async-start(bf16[4,2,512]{2,1,0:T(2,128)(2,1)} %reshape.130), calls=%async_computation | async-start | bytes 16384 | tf_op jit(solution)/shard_map/all_to_all | solution.py:35
  351.0 465.0 %all-reduce.8.cloned.1.call-start = ((), (), s32[]{:S(2)}) async-start(), calls=%async_computation.5 | async-start | bytes 2097152
Sparse Core Ops, SparseCore 0:
  345.0 188.5 all-reduce.5
  636.0 179.9 all-reduce.7
